TPU v7x, 256 devices: a whole 4x4x8 slice. The times are simulated.
256 devices in a mesh: chan: 32 (over x, y, z_lo), win: 8 (over z_hi, core).
Axes of the slice: x: 4, y: 4, z: 8 (z_hi: 4, z_lo: 2; z = z_hi * 2 + z_lo), core: 2. Of those that a mesh axis runs over, the one named last changes fastest.
Arguments:
- records: float32 [32, 1024, 1024], P('win', 'chan'), may hold values from -180 to 180
- sources: int32 [32], replicated, may hold values from 0 to 1023, as said below
Outputs:
- correlations: float32 [32, 256, 1024], P('win', None, 'chan')
Inputs may be any that keep to these rules, and one draw needn't show every extreme that they name: `sources`: source s is one of the channels s * 32 to (s + 1) * 32 - 1; the first source is channel 0 and the last is channel 1024 - 1.
All inputs are finite; a program needn't handle non-finite values.
Results may differ from a plain program's by a relative error of at most 0.00022.
Values sent between devices are 32-bit elements; how exact they have to be, the bound alone decides.
No kernel may reach another device: no remote copies, remote signals or barrier semaphores. Data moves between devices by JAX's collectives and lax.ppermute only.
A program may use at most 64 MiB of HBM per device.

v0:
```python
import math
import jax
import jax.numpy as jnp
from jax import lax
from jax.sharding import PartitionSpec as P

HIGHEST = lax.Precision.HIGHEST
AMPLITUDE_FLOOR = 0.25
WHITE_EPSILON = 1e-06


def fourier_table(length):
    freq_count = length // 2
    freqs = jnp.arange(freq_count, dtype=jnp.int32)[:, None]
    sample_index = jnp.arange(length, dtype=jnp.int32)[None, :]
    angles = (freqs * sample_index % length).astype(jnp.float32) * (2.0 * math.pi / length)
    return jnp.concatenate([jnp.cos(angles), -jnp.sin(angles)], axis=0)


def band_table(freq_count, reach):
    rows_index = jnp.arange(freq_count, dtype=jnp.int32)[:, None]
    cols_index = jnp.arange(freq_count, dtype=jnp.int32)[None, :]
    return (jnp.abs(rows_index - cols_index) <= reach).astype(jnp.float32)


def inverse_table(length, lag_count, first_bin, bin_count, factor):
    freqs = first_bin + jnp.arange(bin_count, dtype=jnp.int32)
    lag_index = jnp.arange(lag_count, dtype=jnp.int32) - lag_count // 2
    angles = (lag_index[:, None] * freqs[None, :] % length).astype(jnp.float32) * (
        2.0 * math.pi / length
    )
    weights = jnp.where(freqs == 0, 1.0, 2.0).astype(jnp.float32)[None, :] * factor
    return jnp.concatenate([weights * jnp.cos(angles), -weights * jnp.sin(angles)], axis=1)


def running_level(padded, time_count, window_span):
    window_total = padded.shape[0]
    chans = padded.shape[2]
    running = jnp.concatenate(
        [jnp.zeros((window_total, 1, chans), jnp.float32), jnp.cumsum(jnp.abs(padded), axis=1)],
        axis=1,
    )
    return (running[:, window_span:] - running[:, :time_count]) / window_span


def local(records, sources):
    chan_count = lax.axis_size("chan")
    local_windows, local_time, all_channels = records.shape
    length = local_time * chan_count
    freq_count = length // 2
    chan_width = all_channels // chan_count
    half_width = min(16, local_time)
    smooth_reach = length // 32
    window_span = 2 * half_width + 1
    lag_count = length // 4
    forward = fourier_table(length)
    band_matrix = band_table(freq_count, smooth_reach)
    pieces = lax.all_to_all(records, "chan", split_axis=2, concat_axis=1, tiled=True)
    padded = jnp.pad(pieces, ((0, 0), (half_width, half_width), (0, 0)))
    amplitude = running_level(padded, length, window_span)
    whiten_pieces = pieces / jnp.maximum(amplitude, AMPLITUDE_FLOOR)
    spectrum = jnp.einsum("kt,wtc->wkc", forward, whiten_pieces, precision=HIGHEST)
    real_part = spectrum[:, :freq_count]
    imag_part = spectrum[:, freq_count:]
    magnitude = jnp.sqrt(real_part * real_part + imag_part * imag_part)
    smoothed = (
        jnp.einsum("jk,wkc->wjc", band_matrix, magnitude, precision=HIGHEST)
        / (2 * smooth_reach + 1)
        + WHITE_EPSILON
    )
    whitened = jnp.stack([real_part / smoothed, imag_part / smoothed], axis=1)
    band_data = lax.all_to_all(whitened, "win", split_axis=2, concat_axis=0, tiled=True)
    total_windows = band_data.shape[0]
    band_count = band_data.shape[2]
    chan_index = lax.axis_index("chan")
    channel_ids = jnp.arange(chan_width, dtype=jnp.int32)
    selector = (sources[:, None] == chan_index * chan_width + channel_ids[None, :]).astype(
        jnp.float32
    )
    chosen = jnp.einsum("sc,wafc->wafs", selector, band_data, precision=HIGHEST)
    spectra = lax.psum(chosen, "chan")
    source_real = spectra[:, 0]
    source_imag = spectra[:, 1]
    white_real = band_data[:, 0]
    white_imag = band_data[:, 1]
    cross_real = jnp.einsum(
        "wfs,wfc->fsc", source_real, white_real, precision=HIGHEST
    ) + jnp.einsum("wfs,wfc->fsc", source_imag, white_imag, precision=HIGHEST)
    cross_imag = jnp.einsum(
        "wfs,wfc->fsc", source_real, white_imag, precision=HIGHEST
    ) - jnp.einsum("wfs,wfc->fsc", source_imag, white_real, precision=HIGHEST)
    stacked = jnp.stack([cross_real, cross_imag])
    factor = 1.0 / math.sqrt(total_windows * freq_count)
    band_start = lax.axis_index("win") * band_count
    band_table_part = inverse_table(length, lag_count, band_start, band_count, factor).reshape(
        lag_count, 2, band_count
    )
    return lax.psum_scatter(
        jnp.einsum("tak,aksc->stc", band_table_part, stacked, precision=HIGHEST),
        "win",
        scatter_dimension=0,
        tiled=True,
    )


def solution(mesh):
    placed = (P("win", "chan", None), P())
    return jax.shard_map(
        local, mesh=mesh, in_specs=placed, out_specs=P("win", None, "chan"), check_vma=False
    )
```

profile of v0, /device:TPU:2, one launch (start us, length us, event | category | flops | bytes accessed | tf_op | source)
XLA Modules:
  0.0 526.2 jit_solution(4063981459503955568)
XLA Ops:
  6.5 1.8 copy.27
  8.3 2.1 reshape.206
  10.4 9.0 %all-to-all-start = ((f32[32,1,4096]{2,1,0:T(1,128)}), f32[32,1,4096]{2,1,0:T(1,128)S(1)}, u32[]{:S(2)}, u32[]{:S(2)}) async-start(f32[32,1,4096]{2,1,0:T(1,128)} %reshape.206), calls=%async_computation | async-start | bytes 1048576 | tf_op jit(solution)/shard_map/all_to_all | solution.py:58
  19.4 9.1 %sine_negate_fusion = (f32[512,1024]{1,0:T(8,128)S(1)}, f32[512,1024]{1,0:T(8,128)}) fusion(), kind=kLoop, calls=%fused_computation.14 | loop fusion | flops 7864320 | bytes 4194304 | tf_op jit(solution)/shard_map/neg | solution.py:17
  28.5 0.7 all-to-all-done
  29.2 0.5 broadcast.250
  29.7 1.9 reduce
  31.6 2.4 reshape.207
  34.0 4.1 copy.49
  38.1 2.4 all_to_all.29
  40.5 0.0 copy-start.1
  40.5 0.2 abs_bitcast_fusion
  40.8 0.5 copy-done.1
  41.3 1.1 reshape.199
  42.4 62.7 %reduce-window.6 = f32[4,32,9,128]{3,2,1,0:T(8,128)S(1)} reduce-window(f32[4,32,9,128]{3,2,1,0:T(8,128)} %reshape.199, f32[]{:T(128)} %constant.22.clone.1), window={size=1x1x1x128 pad=0_0x0_0x0_0x127_0}, to_apply=%region_0.1 | reduce-window | flops 18726912 | bytes 1179652 | tf_op jit(solution)/shard_map/reduce-window
  105.2 1.3 slice.45
  106.5 1.5 copy.29
  108.1 0.1 copy.30
  108.2 1.3 broadcast_add_fusion
  109.5 1.3 reduce_window_sum.16
  110.8 6.1 %fusion.16 = f32[4,1024,32]{1,2,0:T(8,128)S(1)} fusion(f32[512,1024]{1,0:T(8,128)S(1)} %get-tuple-element.13, f32[512,1024]{1,0:T(8,128)} %get-tuple-element.14, f32[4,1024,32]{1,2,0:T(8,128)} %copy-done.1, f32[4,1056,32]{1,2,0:T(8,128)S(1)} %bitcast.85, f32[4,1152,32]{1,2,0:T(8,128)S(1)} %bitcast.84), kind=kOutput, calls=%fused_computation.23 | convolution fusion | flops 1612185600 | bytes 6356992 | tf_op jit(solution)/shard_map/kt,wtc->wkc/dot_general | solution.py:62
  117.0 0.7 divide_bitcast_fusion.1
  117.7 1.3 copy.31
  119.0 2.1 reshape.208
  121.1 7.6 %all-to-all-start.1 = ((f32[8,1,16384]{2,1,0:T(1,128)}), f32[8,1,16384]{2,1,0:T(1,128)S(1)}, u32[]{:S(2)}, u32[]{:S(2)}) async-start(f32[8,1,16384]{2,1,0:T(1,128)} %reshape.208), calls=%async_computation.1 | async-start | bytes 1048576 | tf_op jit(solution)/shard_map/all_to_all | solution.py:72
  128.7 0.0 all-reduce.5.cloned.1.call-start
  128.8 18.3 %all-to-all-done.1 = f32[8,1,16384]{2,1,0:T(1,128)S(1)} async-done(((f32[8,1,16384]{2,1,0:T(1,128)}), f32[8,1,16384]{2,1,0:T(1,128)S(1)}, u32[]{:S(2)}, u32[]{:S(2)}) %all-to-all-start.1) | async-done | bytes 524320 | tf_op jit(solution)/shard_map/all_to_all | solution.py:72
  147.0 1.9 reduce.1
  148.9 1.1 reshape.209
  150.0 0.0 copy-start.2
  150.0 0.8 copy.32
  150.9 0.0 copy-done.2
  150.9 1.6 fusion.44
  152.5 0.0 all-reduce.5.cloned.1.call-update
  152.5 0.0 reduce-scatter.2.cloned.1.call-start
  152.6 0.3 cosine_multiply_fusion
  152.9 0.1 slice_bitcast_fusion.2
  153.0 0.9 copy.34
  154.0 0.9 copy.36
  154.9 299.8 %all-reduce.5.cloned.1.call-done = f32[32,2,64,32]{2,3,1,0:T(8,128)} async-done(((f32[32,2,64,32]{2,3,1,0:T(8,128)}), f32[32,2,64,32]{2,3,1,0:T(8,128)}) %all-reduce.5.cloned.1.call-update) | async-done | bytes 524304 | tf_op jit(solution)/shard_map/psum | solution.py:81
  454.7 2.3 slice_bitcast_fusion.1
  457.0 2.0 copy.33
  459.0 2.8 copy.35
  461.8 1.2 fusion.61
  463.0 0.0 copy-start
  463.0 1.2 fusion.62
  464.2 0.0 copy-done
  464.2 1.2 fusion.15
  465.4 1.2 fusion.14
  466.6 0.3 pad_maximum_fusion
  466.8 5.1 fusion.11
  472.0 0.0 reduce-scatter.2.cloned.1.call-update
  472.0 47.4 %reduce-scatter.2.cloned.1.call-done = f32[4,256,32]{1,2,0:T(8,128)} async-done(((f32[32,256,32]{1,2,0:T(8,128)}), f32[4,256,32]{1,2,0:T(8,128)}) %reduce-scatter.2.cloned.1.call-update) | async-done | bytes 131088 | tf_op jit(solution)/shard_map/reduce_scatter | solution.py:98
  (8 shorter events, 0.1 us)
Async XLA Ops:
  10.4 18.7 %all-to-all-start = ((f32[32,1,4096]{2,1,0:T(1,128)}), f32[32,1,4096]{2,1,0:T(1,128)S(1)}, u32[]{:S(2)}, u32[]{:S(2)}) async-start(f32[32,1,4096]{2,1,0:T(1,128)} %reshape.206), calls=%async_computation | async-start | bytes 1048576 | tf_op jit(solution)/shard_map/all_to_all | solution.py:58
  40.5 0.8 copy-start.1
  121.1 25.9 %all-to-all-start.1 = ((f32[8,1,16384]{2,1,0:T(1,128)}), f32[8,1,16384]{2,1,0:T(1,128)S(1)}, u32[]{:S(2)}, u32[]{:S(2)}) async-start(f32[8,1,16384]{2,1,0:T(1,128)} %reshape.208), calls=%async_computation.1 | async-start | bytes 1048576 | tf_op jit(solution)/shard_map/all_to_all | solution.py:72
  128.7 326.1 %all-reduce.5.cloned.1.call-start = ((), (), s32[]{:S(2)}) async-start(), calls=%async_computation.3 | async-start | bytes 2097152 | tf_op jit(solution)/shard_map/psum | solution.py:81
  150.0 0.8 copy-start.2
  152.5 366.9 %reduce-scatter.2.cloned.1.call-start = ((), (), s32[]{:S(2)}) async-start(), calls=%async_computation.4 | async-start | bytes 1179648 | tf_op jit(solution)/shard_map/reduce_scatter | solution.py:98
  463.0 1.2 copy-start
Sparse Core Ops, SparseCore 0:
  152.7 302.0 all-reduce.4
  472.1 47.2 reduce-scatter.1
where the time goes:
time: 531 us; the launch traced here: 526 us
  waiting for transfers between devices  366 us (69%)
  other arithmetic  77.8 us (15%)
  local copies, waits for them, and re-layouts  33.7 us (6%)
  matrix products  18.3 us (3%)
  starting transfers between devices  16.6 us (3%)
  between operations  13.7 us (3%)
    psum x1, waiting for transfers between devices, local(): spectra = lax.psum(chosen, 'chan')  300 us
    another operation x3, other arithmetic  64.1 us
    reduce_scatter x1, waiting for transfers between devices, local(): lax.psum_scatter(jnp.einsum('tak,aksc->stc', band_table_part, stacked, pr...  47.4 us
    all_to_all x1, waiting for transfers between devices, local(): lax.all_to_all(whitened, 'win', split_axis=2, concat_axis=0, tiled=True)  18.3 us
  transfers between devices with their start and end apart: 4, of which 4 were waited for; matrix products, arithmetic and copies ran while one was open for 2% of the time, Pallas kernels for 0%

commit v1 on v0

--- a/solution.py
+++ b/solution.py
@@ -78,7 +78,7 @@
         jnp.float32
     )
     chosen = jnp.einsum("sc,wafc->wafs", selector, band_data, precision=HIGHEST)
-    spectra = lax.psum(chosen, "chan")
+    spectra = jnp.sum(lax.all_gather(chosen, "chan"), axis=0)
     source_real = spectra[:, 0]
     source_imag = spectra[:, 1]
     white_real = band_data[:, 0]

time: 531 us -> 941 us (1.77)
  waiting for transfers between devices: 366 us -> 764 us
  other arithmetic: 77.8 us -> 91 us
    all_gather x0 -> x1, waiting for transfers between devices: none -> 705 us  [local(): spectra = jnp.sum(lax.all_gather(chosen, 'chan'), axis=0)]
    psum x1 -> x0, waiting for transfers between devices: 300 us -> none  [local(): spectra = lax.psum(chosen, 'chan')]
    reduce_sum x0 -> x1, other arithmetic: none -> 13.2 us  [local(): spectra = jnp.sum(lax.all_gather(chosen, 'chan'), axis=0)]
  transfers between devices with their start and end apart: 4 -> 4, of which waited for: 4 -> 4; matrix products, arithmetic and copies ran while one was open for 2% -> 1% of each run, Pallas kernels for 0% -> 0%
where the time goes in v1:
time: 941 us; the launch traced here: 936 us
  waiting for transfers between devices  764 us (81%)
  other arithmetic  91 us (10%)
  local copies, waits for them, and re-layouts  32.4 us (3%)
  matrix products  18.2 us (2%)
  starting transfers between devices  16.6 us (2%)
  between operations  13.7 us (1%)
    all_gather x1, waiting for transfers between devices, local(): spectra = jnp.sum(lax.all_gather(chosen, 'chan'), axis=0)  705 us
    another operation x3, other arithmetic  64.1 us
    reduce_scatter x1, waiting for transfers between devices, local(): lax.psum_scatter(jnp.einsum('tak,aksc->stc', band_table_part, stacked, pr...  40.4 us
  transfers between devices with their start and end apart: 4, of which 4 were waited for; matrix products, arithmetic and copies ran while one was open for 1% of the time, Pallas kernels for 0%

profile of v1, /device:TPU:2, one launch (start us, length us, event | category | flops | bytes accessed | tf_op | source)
XLA Modules:
  0.0 935.9 jit_solution(351306183709114432)
XLA Ops:
  6.5 1.8 copy.19
  8.3 2.1 reshape.207
  10.4 9.0 all-to-all-start
  19.4 9.1 sine_negate_fusion
  28.5 0.7 all-to-all-done
  29.2 0.5 broadcast.250
  29.7 1.9 reduce
  31.6 2.4 reshape.208
  34.0 4.1 copy.41
  38.1 2.4 all_to_all.29
  40.5 0.0 copy-start.1
  40.5 0.2 abs_bitcast_fusion
  40.8 0.5 copy-done.1
  41.3 1.1 reshape.199
  42.4 62.7 %reduce-window.6 = f32[4,32,9,128]{3,2,1,0:T(8,128)S(1)} reduce-window(f32[4,32,9,128]{3,2,1,0:T(8,128)} %reshape.199, f32[]{:T(128)} %constant.22.clone.1), window={size=1x1x1x128 pad=0_0x0_0x0_0x127_0}, to_apply=%region_0.1 | reduce-window | flops 18726912 | bytes 1179652 | tf_op jit(solution)/shard_map/reduce-window
  105.2 1.3 slice.45
  106.5 1.5 copy.21
  108.1 0.1 copy.22
  108.2 1.3 broadcast_add_fusion
  109.5 1.3 reduce_window_sum.16
  110.8 6.1 fusion.16
  117.0 0.7 divide_bitcast_fusion.1
  117.7 1.3 copy.23
  119.0 2.1 reshape.209
  121.1 7.6 all-to-all-start.1
  128.7 0.0 all-gather.3.cloned.1.call-start
  128.7 18.3 %all-to-all-done.1 = f32[8,1,16384]{2,1,0:T(1,128)S(1)} async-done(((f32[8,1,16384]{2,1,0:T(1,128)}), f32[8,1,16384]{2,1,0:T(1,128)S(1)}, u32[]{:S(2)}, u32[]{:S(2)}) %all-to-all-start.1) | async-done | bytes 524320 | tf_op jit(solution)/shard_map/all_to_all | solution.py:72
  147.0 1.9 reduce.1
  148.9 1.1 reshape.210
  150.0 0.0 copy-start.2
  150.0 0.8 copy.24
  150.9 0.0 copy-done.2
  150.9 1.6 fusion.50
  152.5 0.0 all-gather.3.cloned.1.call-update
  152.5 0.0 reduce-scatter.2.cloned.1.call-start
  152.6 0.3 cosine_multiply_fusion
  152.9 0.1 slice_bitcast_fusion.1
  153.0 0.9 copy.26
  153.9 0.9 copy.28
  154.9 704.6 %all-gather.3.cloned.1.call-done = f32[1024,2,64,32]{2,3,1,0:T(8,128)} async-done(((f32[32,2,64,32]{2,3,1,0:T(8,128)}), f32[1024,2,64,32]{2,3,1,0:T(8,128)}) %all-gather.3.cloned.1.call-update) | async-done | bytes 16777232 | tf_op jit(solution)/shard_map/all_gather | solution.py:81
  859.4 13.2 %reduce_sum.9 = f32[32,2,64,32]{2,3,1,0:T(8,128)S(1)} reduce(f32[32,32,2,64,32]{3,4,2,1,0:T(8,128)} %bitcast.80, f32[]{:T(128)} %constant.22.clone.1), dimensions={0}, to_apply=%region_2.3 | reduce | flops 4063232 | bytes 17301508 | tf_op jit(solution)/shard_map/reduce_sum | solution.py:81
  872.7 1.0 fusion.63
  873.7 2.0 copy.34
  875.7 2.8 copy.35
  878.5 1.2 fusion.23
  879.7 0.0 copy-start
  879.7 1.2 fusion.21
  880.8 0.0 copy-done
  880.9 1.2 fusion.15
  882.1 1.2 fusion.14
  883.2 0.3 pad_maximum_fusion
  883.5 5.1 fusion.11
  888.6 0.0 reduce-scatter.2.cloned.1.call-update
  888.6 40.4 %reduce-scatter.2.cloned.1.call-done = f32[4,256,32]{1,2,0:T(8,128)} async-done(((f32[32,256,32]{1,2,0:T(8,128)}), f32[4,256,32]{1,2,0:T(8,128)}) %reduce-scatter.2.cloned.1.call-update) | async-done | bytes 131088 | tf_op jit(solution)/shard_map/reduce_scatter | solution.py:98
  (8 shorter events, 0.1 us)
Async XLA Ops:
  10.4 18.7 %all-to-all-start = ((f32[32,1,4096]{2,1,0:T(1,128)}), f32[32,1,4096]{2,1,0:T(1,128)S(1)}, u32[]{:S(2)}, u32[]{:S(2)}) async-start(f32[32,1,4096]{2,1,0:T(1,128)} %reshape.207), calls=%async_computation | async-start | bytes 1048576 | tf_op jit(solution)/shard_map/all_to_all | solution.py:58
  40.5 0.8 copy-start.1
  121.1 25.9 %all-to-all-start.1 = ((f32[8,1,16384]{2,1,0:T(1,128)}), f32[8,1,16384]{2,1,0:T(1,128)S(1)}, u32[]{:S(2)}, u32[]{:S(2)}) async-start(f32[8,1,16384]{2,1,0:T(1,128)} %reshape.209), calls=%async_computation.1 | async-start | bytes 1048576 | tf_op jit(solution)/shard_map/all_to_all | solution.py:72
  128.7 730.8 %all-gather.3.cloned.1.call-start = ((), (), s32[]{:S(2)}) async-start(), calls=%async_computation.4 | async-start | bytes 34603008 | tf_op jit(solution)/shard_map/all_gather | solution.py:81
  150.0 0.8 copy-start.2
  152.5 776.6 %reduce-scatter.2.cloned.1.call-start = ((), (), s32[]{:S(2)}) async-start(), calls=%async_computation.3 | async-start | bytes 1179648 | tf_op jit(solution)/shard_map/reduce_scatter | solution.py:98
  879.7 1.2 copy-start
Sparse Core Ops, SparseCore 0:
  152.6 706.7 all-gather.2
  888.8 40.2 reduce-scatter.1
